TPU v7x, 128 devices: a whole 4x4x4 slice. The times are simulated.
128 devices in a mesh: dp: 32 (over z, y, core), col: 4 (over x).
Axes of the slice: x: 4, y: 4, z: 4, core: 2. Of those that a mesh axis runs over, the one named last changes fastest.
Arguments:
- tokens: bfloat16 [32768, 8192], P('dp', 'col'), may hold values from -6 to 6
- out_grad: bfloat16 [32768, 8192], P(('dp', 'col')), may hold values from -24 to 24
- weight: float32 [8192, 8192], P('dp', 'col'), may hold values from -6 to 6
- second: float32 [8192, 8192], P('dp', 'col'), may hold values from 0.0001 to 0.001
- momentum: float32 [8192, 512], P(('dp', 'col')), may hold values from -0.12 to 0.12
- sign_seed: int32 [1], replicated, may hold values from 0 to 999999
- step_number: int32 [1], replicated, may hold values from 1 to 999999
Outputs:
- new_weight: float32 [8192, 8192], P('dp', 'col')
- new_second: float32 [8192, 8192], P('dp', 'col')
- new_momentum: float32 [8192, 512], P(('dp', 'col'))
All inputs are finite; a program needn't handle non-finite values.
Results may differ from a plain program's by a relative error of at most 0.00097.
Values may be sent and summed in bfloat16 or wider, within the bound.
A program may use at most 128 MiB of HBM per device.

v0:
```python
import jax
import jax.numpy as jnp
from jax import lax
from jax.sharding import Mesh
from jax.sharding import PartitionSpec as P

DP = ("dp_0", "dp_1", "dp_2")
DP_COL = ("dp_0", "dp_1", "dp_2", "col")


def split_up(x, dim, count):
    before, after = (x.shape[:dim], x.shape[dim + 1 :])
    return jnp.moveaxis(x.reshape(*before, count, -1, *after), dim, 0)


def sent_and_summed(x, axis, dim):
    count = lax.axis_size(axis)
    pieces = lax.all_to_all(split_up(x, dim, count), axis, 0, 0, tiled=True)
    return jnp.sum(pieces, axis=0)


def from_everyone(x, axis):
    copies = jnp.broadcast_to(x, (lax.axis_size(axis), *x.shape))
    return lax.all_to_all(copies, axis, split_axis=0, concat_axis=0, tiled=True)


def joined_along(pieces, dim):
    pieces = jnp.moveaxis(pieces, 0, dim)
    lengths = pieces.shape
    return pieces.reshape(*lengths[:dim], lengths[dim] * lengths[dim + 1], *lengths[dim + 2 :])


def gather_directly(x, axis, dim):
    pieces = from_everyone(x, axis)
    return joined_along(pieces, dim)


def sum_in_two_steps(x, axes, dim):
    far, near = axes
    own = sent_and_summed(split_up(x, dim, lax.axis_size(far)), near, dim + 1)
    return jnp.sum(lax.all_to_all(own, far, 0, 0, tiled=True), axis=0)


def sign_table(sign_seed, step_number, first_row, row_count, low_rank):
    row_ids = first_row + lax.iota(jnp.int32, row_count)
    col_ids = lax.iota(jnp.int32, low_rank)
    flat_index = row_ids[:, None] * low_rank + col_ids[None, :]
    hashed = flat_index * 747796405 + sign_seed[0] * 1664525 + step_number[0] * 1013904223
    hashed = hashed ^ hashed >> 16 & 65535
    hashed = hashed * 2127912213
    hashed = hashed ^ hashed >> 13 & 524287
    hashed = hashed * 1103515245
    hashed = hashed ^ hashed >> 16 & 65535
    low_bit = hashed >> 20 & 1
    return (1 - 2 * low_bit).astype(jnp.float32)


def contract(left_rows, right_rows):
    return lax.dot_general(
        left_rows, right_rows, (((0,), (0,)), ((), ())), preferred_element_type=jnp.float32
    )


def per_device(tokens, out_grad, weight, second, momentum, sign_seed, step_number):
    local_tokens, din_local = tokens.shape
    low_rank = momentum.shape[1]
    owner_rows = momentum.shape[0]
    inv_root = 1.0 / jnp.sqrt(jnp.float32(low_rank))
    col_position = lax.axis_index("col")
    sign_block = sign_table(sign_seed, step_number, col_position * din_local, din_local, low_rank)
    partial_sketch = (
        jnp.dot(tokens, sign_block.astype(jnp.bfloat16), preferred_element_type=jnp.float32)
        * inv_root
    )
    quarter = sent_and_summed(partial_sketch, "col", 0)
    sketch = quarter.astype(jnp.bfloat16)
    total_tokens = lax.axis_size(DP) * local_tokens
    data_count = lax.axis_size(DP)
    col_count = lax.axis_size("col")
    quarter_rows = out_grad.shape[0]
    grouped = out_grad.reshape(quarter_rows, data_count, col_count, owner_rows)
    grouped = jnp.transpose(grouped, (0, 2, 1, 3)).reshape(
        quarter_rows, col_count, data_count * owner_rows
    )
    regrouped = lax.all_to_all(grouped, "col", split_axis=1, concat_axis=0, tiled=True)
    regrouped = regrouped.reshape(quarter_rows * col_count, data_count * owner_rows)
    shard_sketch = gather_directly(sketch, "col", 0)
    projected = sum_in_two_steps(contract(regrouped, shard_sketch), (("dp_0", "dp_1"), "dp_2"), 0)
    projected = projected / jnp.float32(total_tokens)
    new_momentum = 0.8 * momentum + 0.2 * projected
    row_block = gather_directly(new_momentum, "col", 0)
    dense_grad = (
        lax.dot_general(
            row_block,
            sign_block,
            (((1,), (1,)), ((), ())),
            precision=lax.Precision.HIGHEST,
            preferred_element_type=jnp.float32,
        )
        * inv_root
    )
    new_second = 0.95 * second + 0.05 * dense_grad * dense_grad
    new_weight = weight - 0.5 * dense_grad / (jnp.sqrt(new_second) + 1e-08)
    return (new_weight, new_second, new_momentum)


def solution(mesh):
    torus = Mesh(mesh.devices.reshape(4, 4, 2, mesh.shape["col"]), ("dp_0", "dp_1", "dp_2", "col"))
    return jax.shard_map(
        per_device,
        mesh=torus,
        in_specs=(
            P(DP, "col"),
            P(DP_COL, None),
            P(DP, "col"),
            P(DP, "col"),
            P(DP_COL, None),
            P(),
            P(),
        ),
        out_specs=(P(DP, "col"), P(DP, "col"), P(DP_COL, None)),
        check_vma=False,
    )
```

profile of v0, /device:TPU:0, one launch (start us, length us, event | category | flops | bytes accessed | tf_op | source)
XLA Modules:
  0.0 196.9 jit_solution(12246148960320195151)
XLA Ops:
  1.9 6.4 %fusion.3 = f32[512,1024]{1,0:T(8,128)S(1)} fusion(bf16[1024,2048]{1,0:T(8,128)(2,1)} %param.7, s32[]{:T(128)} %bitcast.1, s32[]{:T(128)} %bitcast, s32[2048]{0:T(1024)S(1)} %add_multiply_fusion), kind=kOutput, calls=%fused_computation.9 | convolution fusion | flops 2170028032 | bytes 6299656 | tf_op jit(solution)/shard_map/dot_general | solution.py:72
  8.3 1.5 copy.33
  9.8 4.4 %all-to-all-start = ((f32[4,256,512]{1,2,0:T(8,128)}), f32[4,256,512]{1,2,0:T(8,128)S(1)}, u32[]{:S(2)}, u32[]{:S(2)}) async-start(f32[4,256,512]{1,2,0:T(8,128)} %bitcast.30), calls=%async_computation | async-start | bytes 4194304 | tf_op jit(solution)/shard_map/all_to_all | solution.py:18
  14.2 6.4 %copy.25 = bf16[256,8192]{0,1:T(8,128)(2,1)} copy(bf16[256,8192]{1,0:T(8,128)(2,1)} %param.8) | data formatting | bytes 8388608 | tf_op args[1]
  20.6 4.7 %copy.26 = bf16[256,4,32,64]{0,3,2,1:T(8,128)(2,1)} copy(bf16[256,4,32,64]{0,3,1,2:T(8,128)(2,1)} %bitcast.29) | data formatting | bytes 8388608 | tf_op jit(solution)/shard_map/transpose | solution.py:82
  25.3 15.2 %all-to-all-done = f32[4,256,512]{1,2,0:T(8,128)S(1)} async-done(((f32[4,256,512]{1,2,0:T(8,128)}), f32[4,256,512]{1,2,0:T(8,128)S(1)}, u32[]{:S(2)}, u32[]{:S(2)}) %all-to-all-start) | async-done | bytes 2097184 | tf_op jit(solution)/shard_map/all_to_all | solution.py:18
  40.5 4.9 %all-to-all-start.2 = ((bf16[256,4,2048]{0,2,1:T(8,128)(2,1)}), bf16[256,4,2048]{0,2,1:T(8,128)(2,1)}, u32[]{:S(2)}, u32[]{:S(2)}) async-start(bf16[256,4,2048]{0,2,1:T(8,128)(2,1)} %bitcast.27), calls=%async_computation.2 | async-start | bytes 8388608 | tf_op jit(solution)/shard_map/all_to_all | solution.py:85
  45.4 0.1 reduce_sum.27
  45.5 0.1 copy.24
  45.7 47.6 %all-to-all-done.2 = bf16[256,4,2048]{0,2,1:T(8,128)(2,1)} async-done(((bf16[256,4,2048]{0,2,1:T(8,128)(2,1)}), bf16[256,4,2048]{0,2,1:T(8,128)(2,1)}, u32[]{:S(2)}, u32[]{:S(2)}) %all-to-all-start.2) | async-done | bytes 4194336 | tf_op jit(solution)/shard_map/all_to_all | solution.py:85
  93.3 1.1 broadcast_in_dim.8
  94.4 3.5 %all-to-all-start.1 = ((bf16[4,256,512]{2,1,0:T(8,128)(2,1)}), bf16[4,256,512]{2,1,0:T(8,128)(2,1)S(1)}, u32[]{:S(2)}, u32[]{:S(2)}) async-start(bf16[4,256,512]{2,1,0:T(8,128)(2,1)} %broadcast_in_dim.8), calls=%async_computation.1 | async-start | bytes 2097152 | tf_op jit(solution)/shard_map/all_to_all | solution.py:24
  97.9 6.3 %copy.27 = bf16[4,256,1,2048]{3,1,0,2:T(8,128)(2,1)} copy(bf16[4,256,1,2048]{1,3,0,2:T(8,128)(2,1)} %bitcast.8) | data formatting | bytes 8388608 | tf_op jit(solution)/shard_map/all_to_all | solution.py:85
  104.2 7.0 %all-to-all-done.1 = bf16[4,256,512]{2,1,0:T(8,128)(2,1)S(1)} async-done(((bf16[4,256,512]{2,1,0:T(8,128)(2,1)}), bf16[4,256,512]{2,1,0:T(8,128)(2,1)S(1)}, u32[]{:S(2)}, u32[]{:S(2)}) %all-to-all-start.1) | async-done | bytes 1048608 | tf_op jit(solution)/shard_map/all_to_all | solution.py:24
  111.1 6.5 %convolution_bitcast_fusion = f32[2048,512]{0,1:T(8,128)} fusion(bf16[1024,512]{1,0:T(8,128)(2,1)S(1)} %bitcast.31, bf16[1024,2048]{1,0:T(8,128)(2,1)} %bitcast.26), kind=kOutput, calls=%fused_computation.4 | convolution fusion | flops 2147483648 | bytes 9437184 | tf_op jit(solution)/shard_map/dot_general | solution.py:59
  117.6 5.4 %copy.28 = f32[2048,512]{1,0:T(8,128)} copy(f32[2048,512]{0,1:T(8,128)} %convolution_bitcast_fusion) | data formatting | bytes 8388608 | tf_op jit(solution)/shard_map/dot_general | solution.py:59
  123.0 2.8 %copy.29 = f32[2,16,64,512]{3,2,1,0:T(8,128)S(1)} copy(f32[2,16,64,512]{3,2,0,1:T(8,128)} %bitcast.28) | data formatting | bytes 8388608 | tf_op jit(solution)/shard_map/transpose | solution.py:13
  125.8 8.2 %all_to_all.40 = f32[2,16,64,512]{3,2,1,0:T(8,128)} all-to-all(f32[2,16,64,512]{3,2,1,0:T(8,128)S(1)} %copy.29), channel_id=1, replica_groups=mesh['dp_0'=4,'dp_1'=4,'dp_2'=2,'col'=4] {'dp_2'}, dimensions={0} | all-to-all | bytes 8388608 | tf_op jit(solution)/shard_map/all_to_all | solution.py:18
  133.9 2.9 %reduce_sum.28 = f32[16,64,512]{2,1,0:T(8,128)S(1)} reduce(f32[2,16,64,512]{3,2,1,0:T(8,128)} %all_to_all.40, f32[]{:T(128)} %constant.21.clone.1), dimensions={0}, to_apply=%region_1.0 | reduce | flops 524288 | bytes 6291460 | tf_op jit(solution)/shard_map/reduce_sum | solution.py:19
  136.8 0.0 copy-start.1
  136.8 36.8 %all_to_all.41 = f32[16,64,512]{2,1,0:T(8,128)} all-to-all(f32[16,64,512]{2,1,0:T(8,128)S(1)} %reduce_sum.28), channel_id=1, replica_groups=mesh['dp_0'=4,'dp_1'=4,'dp_2'=2,'col'=4] {'dp_0','dp_1'}, dimensions={0} | all-to-all | bytes 4194304 | tf_op jit(solution)/shard_map/all_to_all | solution.py:41
  173.6 1.8 reduce_sum.29
  175.3 0.0 copy-done.1
  175.4 0.0 copy-start
  175.4 0.1 broadcast_in_dim.9
  175.5 11.1 %all_to_all.42 = f32[4,64,512]{2,1,0:T(8,128)S(1)} all-to-all(f32[4,64,512]{2,1,0:T(8,128)S(1)} %broadcast_in_dim.9), channel_id=1, replica_groups=mesh['dp_0'=4,'dp_1'=4,'dp_2'=2,'col'=4] {'col'}, dimensions={0} | all-to-all | bytes 1048576 | tf_op jit(solution)/shard_map/all_to_all | solution.py:24
  186.5 10.4 %divide_subtract_fusion = (f32[256,2048]{1,0:T(8,128)}, f32[256,2048]{1,0:T(8,128)}) fusion(f32[256,2048]{1,0:T(8,128)} %param.9, f32[256,2048]{1,0:T(8,128)} %param.10, f32[256,512]{1,0:T(8,128)S(1)} %bitcast.33, s32[]{:T(128)} %bitcast.1, s32[]{:T(128)} %bitcast, s32[2048]{0:T(1024)S(1)} %add_multiply_fusion), kind=kOutput, calls=%fused_computation.7 | convolution fusion | flops 3246915584 | bytes 8921096 | tf_op jit(solution)/shard_map/dot_general | solution.py:93
  196.9 0.0 copy-done
  (2 shorter events, 0.0 us)
Async XLA Ops:
  9.8 30.7 %all-to-all-start = ((f32[4,256,512]{1,2,0:T(8,128)}), f32[4,256,512]{1,2,0:T(8,128)S(1)}, u32[]{:S(2)}, u32[]{:S(2)}) async-start(f32[4,256,512]{1,2,0:T(8,128)} %bitcast.30), calls=%async_computation | async-start | bytes 4194304 | tf_op jit(solution)/shard_map/all_to_all | solution.py:18
  40.5 52.8 %all-to-all-start.2 = ((bf16[256,4,2048]{0,2,1:T(8,128)(2,1)}), bf16[256,4,2048]{0,2,1:T(8,128)(2,1)}, u32[]{:S(2)}, u32[]{:S(2)}) async-start(bf16[256,4,2048]{0,2,1:T(8,128)(2,1)} %bitcast.27), calls=%async_computation.2 | async-start | bytes 8388608 | tf_op jit(solution)/shard_map/all_to_all | solution.py:85
  94.4 16.7 %all-to-all-start.1 = ((bf16[4,256,512]{2,1,0:T(8,128)(2,1)}), bf16[4,256,512]{2,1,0:T(8,128)(2,1)S(1)}, u32[]{:S(2)}, u32[]{:S(2)}) async-start(bf16[4,256,512]{2,1,0:T(8,128)(2,1)} %broadcast_in_dim.8), calls=%async_computation.1 | async-start | bytes 2097152 | tf_op jit(solution)/shard_map/all_to_all | solution.py:24
  136.8 38.5 %copy-start.1 = (f32[64,512]{1,0:T(8,128)S(1)}, f32[64,512]{1,0:T(8,128)}, u32[]{:S(2)}) copy-start(f32[64,512]{1,0:T(8,128)} %param.11) | copy-start | bytes 393220
  175.4 21.6 %copy-start = (f32[64,512]{1,0:T(8,128)}, f32[64,512]{1,0:T(8,128)S(1)}, u32[]{:S(2)}) copy-start(f32[64,512]{1,0:T(8,128)S(1)} %multiply_add_fusion.1) | copy-start | bytes 393220
where the time goes:
time: 198 us; the launch traced here: 197 us
  waiting for transfers between devices  69.8 us (35%)
  blocking collectives  56 us (28%)
  local copies, waits for them, and re-layouts  28.3 us (14%)
  matrix products  23.3 us (12%)
  starting transfers between devices  12.8 us (6%)
  other arithmetic  4.8 us (2%)
  between operations  2.03 us (1%)
    all_to_all x1, waiting for transfers between devices, per_device(): lax.all_to_all(grouped, 'col', split_axis=1, concat_axis=0, tiled=True)  47.6 us
    all_to_all x1, blocking collectives, sum_in_two_steps(): return jnp.sum(lax.all_to_all(own, far, 0, 0, tiled=True), axis=0)  36.8 us
    all_to_all x1, waiting for transfers between devices, sent_and_summed(): pieces = lax.all_to_all(split_up(x, dim, count), axis, 0, 0, tiled=True)  15.2 us
    all_to_all x1, blocking collectives, from_everyone(): return lax.all_to_all(copies, axis, split_axis=0, concat_axis=0, tiled=True)  11.1 us
    dot_general x1, matrix products, per_device(): lax.dot_general(row_block, sign_block, (((1,), (1,)), ((), ())), precisio...  10.4 us
    all_to_all x1, blocking collectives, sent_and_summed(): pieces = lax.all_to_all(split_up(x, dim, count), axis, 0, 0, tiled=True)  8.17 us
    all_to_all x1, waiting for transfers between devices, from_everyone(): return lax.all_to_all(copies, axis, split_axis=0, concat_axis=0, tiled=True)  6.95 us
    dot_general x1, matrix products, contract(): lax.dot_general(left_rows, right_rows, (((0,), (0,)), ((), ())), preferre...  6.5 us
  transfers between devices with their start and end apart: 3, of which 3 were waited for; matrix products, arithmetic and copies ran while one was open for 9% of the time, Pallas kernels for 0%

commit v1 on v0

v1 whole, which is shorter than its diff:
```python
import jax
import jax.numpy as jnp
from jax import lax
from jax.experimental import pallas as pl
from jax.experimental.pallas import tpu as pltpu
from jax.sharding import Mesh
from jax.sharding import PartitionSpec as P

DP = ("z", "y", "c")
DP_COL = ("z", "y", "c", "x")
MESH_ID = pl.DeviceIdType.MESH

RING = 4
RANK = 512
CHUNKS = 4
LANES = 128
TAG = 16
DIN_LOCAL = 2048
QUARTER = 256
TOKENS = 32768
TOP = 16000.0
SLOTS = (2, 1, 3)

INDEX_STEP = 747796405
MIX_ONE = 2127912213
MIX_TWO = 1103515245
HASH_ROWS = 64


def wrapped(value):
    value &= 0xFFFFFFFF
    return value - (1 << 32) if value >= 1 << 31 else value


def ring(axis, step):
    return lax.rem(lax.axis_index(axis) + step, RING)


def coded(values):
    top = jnp.max(jnp.abs(values), axis=(0, 1), keepdims=True)
    exponent = jnp.floor(jnp.log2(jnp.maximum(top, 1e-30)))
    whole = jnp.round(values * (jnp.exp2(-exponent) * TOP)).astype(jnp.int16)
    tag = jnp.broadcast_to(exponent, (TAG, LANES)).astype(jnp.int16)
    return whole, tag


def decoded(ref, rows):
    exponent = ref[rows : rows + TAG, :].astype(jnp.float32)[0:1, :]
    return ref[0:rows, :].astype(jnp.float32) * (jnp.exp2(exponent) * (1.0 / TOP))


def store_coded(ref, rows, values):
    whole, tag = coded(values)
    ref[0:rows, :] = whole
    ref[rows : rows + TAG, :] = tag


def hash_signs(offset, first_row, part, out_ref):
    width = out_ref.shape[2]
    shape = (HASH_ROWS, width)
    base = lax.broadcasted_iota(jnp.int32, shape, 0) * wrapped(RANK * INDEX_STEP)
    base += (lax.broadcasted_iota(jnp.int32, shape, 1) + part * width) * INDEX_STEP

    def body(step, carry):
        row = pl.multiple_of(step * HASH_ROWS, HASH_ROWS)
        mixed = base + (offset + (first_row + row) * wrapped(RANK * INDEX_STEP))
        mixed = mixed ^ lax.shift_right_logical(mixed, jnp.int32(16))
        mixed = mixed * MIX_ONE
        mixed = mixed ^ lax.shift_right_logical(mixed, jnp.int32(13))
        mixed = mixed * wrapped(MIX_TWO << 11)
        out_ref[part, pl.ds(row, HASH_ROWS), :] = jnp.where(mixed < 0, -1.0, 1.0).astype(jnp.bfloat16)
        return carry

    lax.fori_loop(0, out_ref.shape[1] // HASH_ROWS, body, 0)


def reduce_kernel(
    seed_ref, step_ref, tokens_ref, grad_ref, momentum_ref,
    rows_ref, signs_ref,
    tok, sg, s_own, s_send, s_recv, sk, og, og_t,
    p_own, p_send, p_recv, q_own, q_send, q_recv, r_recv, rows,
    tok_sem, og_sem, sg_sem, s_ss, s_rs, sk_ss, sk_rs,
    p_ss, p_rs, q_ss, q_rs, r_ss, r_rs, a_ss, a_rs,
):
    x, y, z, c = (lax.axis_index(name) for name in ("x", "y", "z", "c"))
    other = 1 - c
    first = (("y", "z"), ("z", "y"))

    barrier = pltpu.get_barrier_semaphore()
    for axis in ("x", "y", "z"):
        for step in SLOTS:
            pl.semaphore_signal(barrier, inc=1, device_id={axis: ring(axis, step)}, device_id_type=MESH_ID)
    pl.semaphore_signal(barrier, inc=1, device_id={"c": other}, device_id_type=MESH_ID)

    def remote(src, dst, send_sem, recv_sem, where):
        return pltpu.make_async_remote_copy(
            src_ref=src, dst_ref=dst, send_sem=send_sem, recv_sem=recv_sem, device_id=where, device_id_type=MESH_ID
        )

    tok_copies = {}
    for place, step in enumerate((2, 1, 3, 0)):
        at = pl.ds(pl.multiple_of(ring("x", step) * QUARTER, QUARTER), QUARTER)
        tok_copies[step] = pltpu.make_async_copy(tokens_ref.at[at], tok.at[at], tok_sem.at[place])
        tok_copies[step].start()
    mine = pl.ds(pl.multiple_of(c * QUARTER, QUARTER), QUARTER)
    theirs = pl.ds(pl.multiple_of(other * QUARTER, QUARTER), QUARTER)

    def columns(block, core):
        return pl.ds(pl.multiple_of((block * 2 + core) * 256, 256), 256)

    def start_own(block, carry):
        pltpu.make_async_copy(grad_ref.at[:, columns(block, c)], og.at[block, mine], og_sem.at[0]).start()
        return carry

    lax.fori_loop(0, 16, start_own, 0)

    offset = seed_ref[0] * 1664525 + step_ref[0] * 1013904223
    hash_signs(offset, x * DIN_LOCAL, 0, sg)

    pl.semaphore_wait(barrier, 10)

    def start_swap(block, carry):
        remote(grad_ref.at[:, columns(block, other)], og.at[block, mine], og_sem.at[1], og_sem.at[2], {"c": other}).start()
        return carry

    lax.fori_loop(0, 16, start_swap, 0)

    pending = []

    for pair in range(2):
        if pair:
            hash_signs(offset, x * DIN_LOCAL, 1, sg)
            signs_out = pltpu.make_async_copy(sg, signs_ref, sg_sem)
            signs_out.start()
        for step in (2, 1, 3, 0):
            if not pair:
                tok_copies[step].wait()
            at = pl.ds(pl.multiple_of(ring("x", step) * QUARTER, QUARTER), QUARTER)
            part = jnp.dot(tok[at, :], sg[pair], preferred_element_type=jnp.float32)
            for half in range(2):
                k = pair * 2 + half
                values = part[:, half * LANES : (half + 1) * LANES]
                if step == 0:
                    s_own[k] = values
                else:
                    slot = step - 1
                    store_coded(s_send.at[k, slot], QUARTER, values)
                    copy = remote(
                        s_send.at[k, slot], s_recv.at[k, slot], s_ss.at[k, slot], s_rs.at[k, slot], {"x": ring("x", step)}
                    )
                    copy.start()
                    pending.append(copy)

    pltpu.make_async_copy(og.at[:, mine], og.at[:, mine], og_sem.at[0]).wait()
    swap = remote(og.at[:, mine], og.at[:, theirs], og_sem.at[1], og_sem.at[2], {"c": other})
    swap.wait_recv()

    def turn(block, carry):
        turned = og[block].T
        at_z = block // 4
        at_y = lax.rem(block, 4)
        for peer in range(RING):
            og_t[0, at_y, pl.ds(pl.multiple_of(peer * 128 + at_z * 32, 32), 32), :] = turned[peer * 64 : peer * 64 + 32]
            og_t[1, at_z, pl.ds(pl.multiple_of(peer * 128 + at_y * 32, 32), 32), :] = turned[peer * 64 + 32 : peer * 64 + 64]
        return carry

    lax.fori_loop(0, 16, turn, 0)

    def sketch(k):
        total = s_own[k]
        for slot in range(3):
            pltpu.make_async_copy(s_recv.at[k, slot], s_recv.at[k, slot], s_rs.at[k, slot]).wait()
            total += decoded(s_recv.at[k, slot], QUARTER)
        sk[k, mine, :] = (total * (1.0 / jnp.sqrt(jnp.float32(RANK)))).astype(jnp.bfloat16)
        copy = remote(sk.at[k, mine], sk.at[k, mine], sk_ss.at[k], sk_rs.at[k], {"c": other})
        copy.start()
        pending.append(copy)

    def phase_one(k):
        pltpu.make_async_copy(sk.at[k, theirs], sk.at[k, theirs], sk_rs.at[k]).wait()
        right = sk[k]
        for step in (2, 1, 3, 0):
            for h, (axis, _) in enumerate(first):
                part = jnp.dot(og_t[h, ring(axis, step)], right, preferred_element_type=jnp.float32)
                if step == 0:
                    p_own[k, h] = part
                else:
                    slot = step - 1
                    store_coded(p_send.at[k, h, slot], 512, part)
                    copy = remote(
                        p_send.at[k, h, slot], p_recv.at[k, h, slot], p_ss.at[k, h, slot], p_rs.at[k, h, slot],
                        {axis: ring(axis, step)},
                    )
                    copy.start()
                    pending.append(copy)

    def phase_two(k):
        for h in range(2):
            total = p_own[k, h]
            for slot in range(3):
                pltpu.make_async_copy(p_recv.at[k, h, slot], p_recv.at[k, h, slot], p_rs.at[k, h, slot]).wait()
                total += decoded(p_recv.at[k, h, slot], 512)
            p_own[k, h] = total
            for step in (2, 1, 3, 0):
                values = p_own[k, h, pl.ds(pl.multiple_of(ring("x", step) * 128, 128), 128), :]
                if step == 0:
                    q_own[k, h] = values
                else:
                    slot = step - 1
                    store_coded(q_send.at[k, h, slot], 128, values)
                    copy = remote(
                        q_send.at[k, h, slot], q_recv.at[k, h, slot], q_ss.at[k, h, slot], q_rs.at[k, h, slot],
                        {"x": ring("x", step)},
                    )
                    copy.start()
                    pending.append(copy)

    def phase_three(k):
        for h, (_, axis) in enumerate(first):
            total = q_own[k, h]
            for slot in range(3):
                pltpu.make_async_copy(q_recv.at[k, h, slot], q_recv.at[k, h, slot], q_rs.at[k, h, slot]).wait()
                total += decoded(q_recv.at[k, h, slot], 128)
            q_own[k, h] = total
            for step in SLOTS:
                slot = step - 1
                copy = remote(
                    q_own.at[k, h, pl.ds(pl.multiple_of(ring(axis, step) * 32, 32), 32)],
                    r_recv.at[k, h, slot], r_ss.at[k, h, slot], r_rs.at[k, h, slot], {axis: ring(axis, step)},
                )
                copy.start()
                pending.append(copy)

    def finish(k):
        for h, (_, axis) in enumerate(first):
            total = q_own[k, h, pl.ds(pl.multiple_of(lax.axis_index(axis) * 32, 32), 32), :]
            for slot in range(3):
                pltpu.make_async_copy(r_recv.at[k, h, slot], r_recv.at[k, h, slot], r_rs.at[k, h, slot]).wait()
                total += r_recv[k, h, slot]
            projected = total * (1.0 / TOKENS)
            old = momentum_ref[h * 32 : h * 32 + 32, k * LANES : (k + 1) * LANES]
            rows[k, pl.ds(pl.multiple_of(x * 64 + h * 32, 32), 32), :] = 0.8 * old + 0.2 * projected
        at = pl.ds(pl.multiple_of(x * 64, 64), 64)
        for step in SLOTS:
            slot = step - 1
            copy = remote(rows.at[k, at], rows.at[k, at], a_ss.at[k, slot], a_rs.at[k, slot], {"x": ring("x", step)})
            copy.start()
            pending.append(copy)

    for k in range(CHUNKS):
        sketch(k)
        phase_one(k)
    phase_two(0)
    phase_three(0)
    phase_two(1)
    finish(0)
    phase_three(1)
    phase_two(2)
    finish(1)
    phase_three(2)
    phase_two(3)
    finish(2)
    phase_three(3)
    finish(3)

    for k in range(CHUNKS):
        for step in SLOTS:
            at = pl.ds(pl.multiple_of(ring("x", RING - step) * 64, 64), 64)
            pltpu.make_async_copy(rows.at[k, at], rows.at[k, at], a_rs.at[k, step - 1]).wait()
        rows_ref[k] = rows[k]
    swap.wait_send()
    signs_out.wait()
    for copy in pending:
        copy.wait_send()


def reduced(sign_seed, step_number, tokens, out_grad, momentum):
    f32, bf16, i16 = jnp.float32, jnp.bfloat16, jnp.int16
    dma = pltpu.SemaphoreType.DMA
    smem = pl.BlockSpec(memory_space=pltpu.SMEM)
    anywhere = pl.BlockSpec(memory_space=pl.ANY)
    vmem = pl.BlockSpec(memory_space=pltpu.VMEM)
    return pl.pallas_call(
        reduce_kernel,
        out_shape=(
            jax.ShapeDtypeStruct((CHUNKS, 256, LANES), f32),
            jax.ShapeDtypeStruct((2, DIN_LOCAL, 256), bf16),
        ),
        in_specs=[smem, smem, anywhere, anywhere, vmem],
        out_specs=(vmem, anywhere),
        scratch_shapes=[
            pltpu.VMEM((1024, DIN_LOCAL), bf16),
            pltpu.VMEM((2, DIN_LOCAL, 256), bf16),
            pltpu.VMEM((CHUNKS, QUARTER, LANES), f32),
            pltpu.VMEM((CHUNKS, 3, QUARTER + TAG, LANES), i16),
            pltpu.VMEM((CHUNKS, 3, QUARTER + TAG, LANES), i16),
            pltpu.VMEM((CHUNKS, 512, LANES), bf16),
            pltpu.VMEM((16, 512, 256), bf16),
            pltpu.VMEM((2, RING, 512, 512), bf16),
            pltpu.VMEM((CHUNKS, 2, 512, LANES), f32),
            pltpu.VMEM((CHUNKS, 2, 3, 512 + TAG, LANES), i16),
            pltpu.VMEM((CHUNKS, 2, 3, 512 + TAG, LANES), i16),
            pltpu.VMEM((CHUNKS, 2, 128, LANES), f32),
            pltpu.VMEM((CHUNKS, 2, 3, 128 + TAG, LANES), i16),
            pltpu.VMEM((CHUNKS, 2, 3, 128 + TAG, LANES), i16),
            pltpu.VMEM((CHUNKS, 2, 3, 32, LANES), f32),
            pltpu.VMEM((CHUNKS, 256, LANES), f32),
            dma((4,)), dma((3,)), dma,
            dma((CHUNKS, 3)), dma((CHUNKS, 3)), dma((CHUNKS,)), dma((CHUNKS,)),
            dma((CHUNKS, 2, 3)), dma((CHUNKS, 2, 3)),
            dma((CHUNKS, 2, 3)), dma((CHUNKS, 2, 3)),
            dma((CHUNKS, 2, 3)), dma((CHUNKS, 2, 3)),
            dma((CHUNKS, 3)), dma((CHUNKS, 3)),
        ],
        compiler_params=pltpu.CompilerParams(
            collective_id=0, has_side_effects=True, vmem_limit_bytes=48 * 1024 * 1024
        ),
        name="sketch_and_reduce",
    )(sign_seed, step_number, tokens, out_grad, momentum)


COLUMNS = 512


def update_kernel(rows_ref, signs_ref, weight_ref, second_ref, new_weight_ref, new_second_ref, momentum_ref, high, low):
    @pl.when(pl.program_id(0) == 0)
    def _():
        mine = pl.ds(pl.multiple_of(lax.axis_index("x") * 64, 64), 64)
        for k in range(CHUNKS):
            values = rows_ref[k]
            top = values.astype(jnp.bfloat16)
            high[:, k * LANES : (k + 1) * LANES] = top
            low[:, k * LANES : (k + 1) * LANES] = (values - top.astype(jnp.float32)).astype(jnp.bfloat16)
            momentum_ref[:, k * LANES : (k + 1) * LANES] = rows_ref[k, mine, :]

    grad = jnp.zeros((256, COLUMNS), jnp.float32)
    for part in range(2):
        at = slice(part * 256, (part + 1) * 256)
        for left in (high, low):
            grad += lax.dot_general(
                left[:, at], signs_ref[part], (((1,), (1,)), ((), ())), preferred_element_type=jnp.float32
            )
    grad = grad * (1.0 / jnp.sqrt(jnp.float32(RANK)))
    second = 0.95 * second_ref[...] + 0.05 * grad * grad
    new_second_ref[...] = second
    new_weight_ref[...] = weight_ref[...] - 0.5 * grad / (jnp.sqrt(second) + 1e-08)


def updated(rows, signs, weight, second):
    f32 = jnp.float32
    tile = pl.BlockSpec((256, COLUMNS), lambda j: (0, j))
    return pl.pallas_call(
        update_kernel,
        grid=(DIN_LOCAL // COLUMNS,),
        out_shape=(
            jax.ShapeDtypeStruct(weight.shape, f32),
            jax.ShapeDtypeStruct(second.shape, f32),
            jax.ShapeDtypeStruct((64, RANK), f32),
        ),
        in_specs=[
            pl.BlockSpec((CHUNKS, 256, LANES), lambda j: (0, 0, 0)),
            pl.BlockSpec((2, COLUMNS, 256), lambda j: (0, j, 0)),
            tile,
            tile,
        ],
        out_specs=(tile, tile, pl.BlockSpec((64, RANK), lambda j: (0, 0))),
        scratch_shapes=[pltpu.VMEM((256, RANK), jnp.bfloat16), pltpu.VMEM((256, RANK), jnp.bfloat16)],
        compiler_params=pltpu.CompilerParams(vmem_limit_bytes=32 * 1024 * 1024),
        name="dense_update",
    )(rows, signs, weight, second)


def per_device(tokens, out_grad, weight, second, momentum, sign_seed, step_number):
    rows, signs = reduced(sign_seed, step_number, tokens, out_grad, momentum)
    return updated(rows, signs, weight, second)


def solution(mesh):
    torus = Mesh(mesh.devices.reshape(4, 4, 2, mesh.shape["col"]), ("z", "y", "c", "x"))
    return jax.shard_map(
        per_device,
        mesh=torus,
        in_specs=(
            P(DP, "x"),
            P(DP_COL, None),
            P(DP, "x"),
            P(DP, "x"),
            P(DP_COL, None),
            P(),
            P(),
        ),
        out_specs=(P(DP, "x"), P(DP, "x"), P(DP_COL, None)),
        check_vma=False,
    )
```

time: 198 us -> 75.4 us (0.38)
  Pallas kernels: 0 us -> 72.4 us
  waiting for transfers between devices: 69.8 us -> 0 us
  blocking collectives: 56 us -> 0 us
  local copies, waits for them, and re-layouts: 28.3 us -> 0.9 us
  matrix products: 23.3 us -> 0 us
  starting transfers between devices: 12.8 us -> 0 us
  other arithmetic: 4.8 us -> 0 us
    pallas_call x0 -> x2, Pallas kernels: none -> 72.4 us  [the longest x1 67.9 us: reduced(): pl.pallas_call(reduce_kernel, out_shape=(jax.ShapeDtypeStruct((CHUNKS, 25...]
    all_to_all x3 -> x0, waiting for transfers between devices: 69.8 us -> none  [the longest x1 47.6 us: per_device(): lax.all_to_all(grouped, 'col', split_axis=1, concat_axis=0, tiled=True)]
    all_to_all x3 -> x0, blocking collectives: 56 us -> none  [the longest x1 36.8 us: sum_in_two_steps(): return jnp.sum(lax.all_to_all(own, far, 0, 0, tiled=True), axis=0)]
    dot_general x3 -> x0, matrix products: 23.3 us -> none  [the longest x1 10.4 us: per_device(): lax.dot_general(row_block, sign_block, (((1,), (1,)), ((), ())), precisio...]
    all_to_all x3 -> x0, starting transfers between devices: 12.8 us -> none  [the longest x1 4.85 us: per_device(): lax.all_to_all(grouped, 'col', split_axis=1, concat_axis=0, tiled=True)]
    transpose x2 -> x0, local copies, waits for them, and re-layouts: 7.49 us -> none  [the longest x1 4.74 us: per_device(): jnp.transpose(grouped, (0, 2, 1, 3))]
    all_to_all x1 -> x0, local copies, waits for them, and re-layouts: 6.26 us -> none  [per_device(): lax.all_to_all(grouped, 'col', split_axis=1, concat_axis=0, tiled=True)]
    unnamed x5 -> x6, local copies, waits for them, and re-layouts: 6.39 us -> 0.9 us
  transfers between devices with their start and end apart: 3 -> 0, of which waited for: 3 -> 0; matrix products, arithmetic and copies ran while one was open for 9% -> 0% of each run, Pallas kernels for 0% -> 0%
where the time goes in v1:
time: 75.4 us; the launch traced here: 75.3 us
  Pallas kernels  72.4 us (96%)
  between operations  1.96 us (3%)
  local copies, waits for them, and re-layouts  0.9 us (1%)
    pallas_call x1, Pallas kernels, reduced(): pl.pallas_call(reduce_kernel, out_shape=(jax.ShapeDtypeStruct((CHUNKS, 25...  67.9 us
    pallas_call x1, Pallas kernels, updated(): pl.pallas_call(update_kernel, grid=(DIN_LOCAL // COLUMNS,), out_shape=(ja...  4.49 us

profile of v1, /device:TPU:0, one launch (start us, length us, event | category | flops | bytes accessed | tf_op | source)
XLA Modules:
  0.0 75.3 jit_solution(9507044897464047417)
XLA Ops:
  1.9 0.0 copy-start.2
  1.9 0.9 %copy-done.2 = f32[64,512]{1,0:T(8,128)S(1)} copy-done((f32[64,512]{1,0:T(8,128)S(1)}, f32[64,512]{1,0:T(8,128)}, u32[]{:S(2)}) %copy-start.2) | copy-done | bytes 131096
  2.8 0.0 copy-start
  2.8 0.0 copy-start.1
  2.8 67.9 %sketch_and_reduce.1 = (f32[4,256,128]{2,1,0:T(8,128)S(1)}, bf16[2,2048,256]{2,1,0:T(8,128)(2,1)S(1)}) custom-call(s32[1]{0:T(128)S(6)} %copy.10.seed_ref, s32[1]{0:T(128)S(6)} %copy.11.step_ref, bf16[1024,2048]{1,0:T(8,128)(2,1)} %tokens_ref.1, bf16[256,8192]{1,0:T(8,128)(2,1)} %grad_ref.1, f32[64,512]{1,0:T(8,128)S(1)} %copy-done.2), custom_call_target="tpu_custom_call" | custom-call | tf_op jit(solution)/shard_map/sketch_and_reduce/pallas_call | solution.py:283
  70.8 0.0 copy-done
  70.8 0.0 copy-done.1
  70.8 4.5 %dense_update.1 = (f32[256,2048]{1,0:T(8,128)}, f32[256,2048]{1,0:T(8,128)}, f32[64,512]{1,0:T(8,128)}) custom-call(f32[4,256,128]{2,1,0:T(8,128)S(1)} %get-tuple-element.5.rows_ref, bf16[2,2048,256]{2,1,0:T(8,128)(2,1)S(1)} %get-tuple-element.6.signs_ref, f32[256,2048]{1,0:T(8,128)S(1)} %copy-done, f32[256,2048]{1,0:T(8,128)S(1)} %copy-done.1), custom_call_target="tpu_custom_call" | custom-call | tf_op jit(solution)/shard_map/dense_update/pallas_call | solution.py:352
Async XLA Ops:
  1.9 0.9 %copy-start.2 = (f32[64,512]{1,0:T(8,128)S(1)}, f32[64,512]{1,0:T(8,128)}, u32[]{:S(2)}) copy-start(f32[64,512]{1,0:T(8,128)} %momentum_ref.1) | copy-start | bytes 393220
  2.8 67.9 %copy-start = (f32[256,2048]{1,0:T(8,128)S(1)}, f32[256,2048]{1,0:T(8,128)}, u32[]{:S(2)}) copy-start(f32[256,2048]{1,0:T(8,128)} %weight_ref.1) | copy-start | bytes 6291460
  2.8 67.9 %copy-start.1 = (f32[256,2048]{1,0:T(8,128)S(1)}, f32[256,2048]{1,0:T(8,128)}, u32[]{:S(2)}) copy-start(f32[256,2048]{1,0:T(8,128)} %second_ref.1) | copy-start | bytes 6291460

commit v2 on v1

v2 whole, which is shorter than its diff:
```python
import jax
import jax.numpy as jnp
from jax import lax
from jax.experimental import pallas as pl
from jax.experimental.pallas import tpu as pltpu
from jax.sharding import Mesh
from jax.sharding import PartitionSpec as P

DP = ("z", "y", "c")
DP_COL = ("z", "y", "c", "x")
MESH_ID = pl.DeviceIdType.MESH

RING = 4
RANK = 512
CHUNKS = 4
LANES = 128
TAG = 16
DIN_LOCAL = 2048
QUARTER = 256
TOKENS = 32768
TOP = 16000.0
SLOTS = (2, 1, 3)

INDEX_STEP = 747796405
MIX_ONE = 2127912213
MIX_TWO = 1103515245
HASH_ROWS = 64


PLAN = (
    ("partial_sketch", 0),
    ("partial_sketch", 1),
    ("sketch", 0),
    ("turn", 0),
    ("phase_one", 0),
    ("sketch", 1),
    ("phase_one", 1),
    ("sketch", 2),
    ("relay", 0),
    ("phase_one", 2),
    ("sketch", 3),
    ("relay", 1),
    ("phase_one", 3),
    ("relay", 2),
    ("phase_two", 0),
    ("relay", 3),
    ("phase_two", 1),
    ("phase_three", 0),
    ("phase_two", 2),
    ("phase_three", 1),
    ("phase_two", 3),
    ("phase_three", 2),
    ("finish", 0),
    ("finish", 1),
    ("phase_three", 3),
    ("finish", 2),
    ("finish", 3),
)


def wrapped(value):
    value &= 0xFFFFFFFF
    return value - (1 << 32) if value >= 1 << 31 else value


def ring(axis, step):
    return lax.rem(lax.axis_index(axis) + step, RING)


def coded(values):
    top = jnp.max(jnp.abs(values), axis=(0, 1), keepdims=True)
    exponent = jnp.floor(jnp.log2(jnp.maximum(top, 1e-30)))
    whole = jnp.round(values * (jnp.exp2(-exponent) * TOP)).astype(jnp.int16)
    tag = jnp.broadcast_to(exponent, (TAG, LANES)).astype(jnp.int16)
    return whole, tag


def decoded(ref, rows):
    exponent = ref[rows : rows + TAG, :].astype(jnp.float32)[0:1, :]
    return ref[0:rows, :].astype(jnp.float32) * (jnp.exp2(exponent) * (1.0 / TOP))


def store_coded(ref, rows, values):
    whole, tag = coded(values)
    ref[0:rows, :] = whole
    ref[rows : rows + TAG, :] = tag


def hash_signs(offset, first_row, part, out_ref):
    width = out_ref.shape[2]
    shape = (HASH_ROWS, width)
    base = lax.broadcasted_iota(jnp.int32, shape, 0) * wrapped(RANK * INDEX_STEP)
    base += (lax.broadcasted_iota(jnp.int32, shape, 1) + part * width) * INDEX_STEP

    def body(step, carry):
        row = pl.multiple_of(step * HASH_ROWS, HASH_ROWS)
        mixed = base + (offset + (first_row + row) * wrapped(RANK * INDEX_STEP))
        mixed = mixed ^ lax.shift_right_logical(mixed, jnp.int32(16))
        mixed = mixed * MIX_ONE
        mixed = mixed ^ lax.shift_right_logical(mixed, jnp.int32(13))
        mixed = mixed * wrapped(MIX_TWO << 11)
        out_ref[part, pl.ds(row, HASH_ROWS), :] = jnp.where(mixed < 0, -1.0, 1.0).astype(jnp.bfloat16)
        return carry

    lax.fori_loop(0, out_ref.shape[1] // HASH_ROWS, body, 0)


def reduce_kernel(
    seed_ref, step_ref, tokens_ref, grad_ref, momentum_ref,
    rows_ref, signs_ref,
    old, tok, sg, s_own, s_send, s_recv, sk, og, og_t,
    p_own, p_send, p_recv, q_own, q_send, q_recv, u_send, u_recv, t_send, t_recv,
    old_sem, tok_sem, og_sem, sg_sem, s_ss, s_rs, sk_ss, sk_rs,
    u_ss, u_rs, p_ss, p_rs, q_ss, q_rs, t_ss, t_rs,
):
    x, y, z, c = (lax.axis_index(name) for name in ("x", "y", "z", "c"))
    other = 1 - c
    first = (("y", "z"), ("z", "y"))

    barrier = pltpu.get_barrier_semaphore()
    for axis in ("x", "y", "z"):
        for step in SLOTS:
            pl.semaphore_signal(barrier, inc=1, device_id={axis: ring(axis, step)}, device_id_type=MESH_ID)
    pl.semaphore_signal(barrier, inc=1, device_id={"c": other}, device_id_type=MESH_ID)

    sems = {
        "s": (s_ss, s_rs), "k": (sk_ss, sk_rs), "u": (u_ss, u_rs), "p": (p_ss, p_rs), "q": (q_ss, q_rs), "t": (t_ss, t_rs)
    }
    sent = {}
    unsent = []

    def remote(src, dst, send_sem, recv_sem, where):
        return pltpu.make_async_remote_copy(
            src_ref=src, dst_ref=dst, send_sem=send_sem, recv_sem=recv_sem, device_id=where, device_id_type=MESH_ID
        )

    def send(kind, at, src, dst, where):
        out, into = sems[kind]
        copy = remote(src, dst, out.at[at], into.at[at], where)
        copy.start()
        sent[kind, at] = copy
        unsent.append((kind, at))

    def left(kind, at):
        sent[kind, at].wait_send()
        unsent.remove((kind, at))

    def arrived(kind, at, ref):
        pltpu.make_async_copy(ref, ref, sems[kind][1].at[at]).wait()

    tok_copies = {}
    for place, step in enumerate((2, 1, 3, 0)):
        at = pl.ds(pl.multiple_of(ring("x", step) * QUARTER, QUARTER), QUARTER)
        tok_copies[step] = pltpu.make_async_copy(tokens_ref.at[at], tok.at[at], tok_sem.at[place])
        tok_copies[step].start()
    mine = pl.ds(pl.multiple_of(c * QUARTER, QUARTER), QUARTER)
    theirs = pl.ds(pl.multiple_of(other * QUARTER, QUARTER), QUARTER)

    def columns(block, core):
        return pl.ds(pl.multiple_of((block * 2 + core) * 256, 256), 256)

    def start_own(block, carry):
        pltpu.make_async_copy(grad_ref.at[:, columns(block, c)], og.at[block, mine], og_sem.at[0]).start()
        return carry

    lax.fori_loop(0, 16, start_own, 0)
    old_copy = pltpu.make_async_copy(momentum_ref, old, old_sem)
    old_copy.start()

    offset = seed_ref[0] * 1664525 + step_ref[0] * 1013904223
    hash_signs(offset, x * DIN_LOCAL, 0, sg)

    pl.semaphore_wait(barrier, 10)

    def start_swap(block, carry):
        remote(grad_ref.at[:, columns(block, other)], og.at[block, mine], og_sem.at[1], og_sem.at[2], {"c": other}).start()
        return carry

    lax.fori_loop(0, 16, start_swap, 0)

    def partial_sketch(pair):
        def send_coded(k, step, values):
            slot = step - 1
            store_coded(s_send.at[k, slot], QUARTER, values)
            send("s", (k, slot), s_send.at[k, slot], s_recv.at[k, slot], {"x": ring("x", step)})

        if pair:
            hash_signs(offset, x * DIN_LOCAL, 1, sg)
            signs_out.start()
        for step in (2, 1, 3, 0):
            if not pair:
                tok_copies[step].wait()
            at = pl.ds(pl.multiple_of(ring("x", step) * QUARTER, QUARTER), QUARTER)
            part = jnp.dot(tok[at, :], sg[pair], preferred_element_type=jnp.float32)
            s_own[2 * pair + 1, step] = part[:, LANES:]
            if step:
                send_coded(2 * pair, step, part[:, :LANES])
            else:
                s_own[2 * pair, step] = part[:, :LANES]
        for step in SLOTS:
            send_coded(2 * pair + 1, step, s_own[2 * pair + 1, step])

    def turn(_):
        pltpu.make_async_copy(og.at[:, mine], og.at[:, mine], og_sem.at[0]).wait()
        swap.wait_recv()

        def body(block, carry):
            turned = og[block].T
            at_z = block // 4
            at_y = lax.rem(block, 4)
            for peer in range(RING):
                row = peer * 64
                og_t[0, at_y, pl.ds(pl.multiple_of(peer * 128 + at_z * 32, 32), 32), :] = turned[row : row + 32]
                og_t[1, at_z, pl.ds(pl.multiple_of(peer * 128 + at_y * 32, 32), 32), :] = turned[row + 32 : row + 64]
            return carry

        lax.fori_loop(0, 16, body, 0)

    def sketch(k):
        total = s_own[k, 0]
        for slot in range(3):
            arrived("s", (k, slot), s_recv.at[k, slot])
            total += decoded(s_recv.at[k, slot], QUARTER)
        sk[k, mine, :] = (total * (1.0 / jnp.sqrt(jnp.float32(RANK)))).astype(jnp.bfloat16)
        send("k", (k,), sk.at[k, mine], sk.at[k, mine], {"c": other})

    def phase_one(k):
        arrived("k", (k,), sk.at[k, theirs])
        right = sk[k]
        for step in (2, 1, 3, 0):
            for h, (axis, _) in enumerate(first):
                part = jnp.dot(og_t[h, ring(axis, step)], right, preferred_element_type=jnp.float32)
                if step == 2:
                    for side, near in enumerate((1, 3)):
                        ref = u_send.at[k, h, side]
                        store_coded(ref, 256, part[side * 256 : side * 256 + 256])
                        send("u", (k, h, side), ref, u_recv.at[k, h, side], {axis: ring(axis, near)})
                else:
                    p_own[k, h, (0, 1, None, 2)[step]] = part

    def relay(k):
        for side, near in enumerate((1, 3)):
            for h, (axis, _) in enumerate(first):
                arrived("u", (k, h, side), u_recv.at[k, h, side])
                rows_at = slice(side * 256, side * 256 + 256)
                p_own[k, h, side + 1, rows_at] += decoded(u_recv.at[k, h, side], 256)
                store_coded(p_send.at[k, h, side], 512, p_own[k, h, side + 1])
                send("p", (k, h, side), p_send.at[k, h, side], p_recv.at[k, h, side], {axis: ring(axis, near)})

    def phase_two(k):
        for h, (_, axis) in enumerate(first):
            total = p_own[k, h, 0]
            for side in range(2):
                arrived("p", (k, h, side), p_recv.at[k, h, side])
                total += decoded(p_recv.at[k, h, side], 512)
            p_own[k, h, 0] = total
            for step in (2, 1, 3, 0):
                at = [pl.ds(pl.multiple_of(peer * 128 + ring(axis, step) * 32, 32), 32) for peer in range(RING)]
                values = jnp.concatenate([p_own[k, h, 0, rows_at, :] for rows_at in at], axis=0)
                if step == 0:
                    q_own[k, h * 128 : h * 128 + 128] = values
                else:
                    slot = step - 1
                    store_coded(q_send.at[k, h, slot], 128, values)
                    send("q", (k, h, slot), q_send.at[k, h, slot], q_recv.at[k, h, slot], {axis: ring(axis, step)})

    def phase_three(k):
        if k == 0:
            old_copy.wait()
        for h in range(2):
            total = q_own[k, h * 128 : h * 128 + 128]
            for slot in range(3):
                arrived("q", (k, h, slot), q_recv.at[k, h, slot])
                total += decoded(q_recv.at[k, h, slot], 128)
            q_own[k, h * 128 : h * 128 + 128] = total * (0.2 / TOKENS)
            at = pl.ds(pl.multiple_of(h * 128 + x * 32, 32), 32)
            q_own[k, at, :] += 0.8 * old[h * 32 : h * 32 + 32, k * LANES : (k + 1) * LANES]
        store_coded(t_send.at[k], 256, q_own[k])
        for step in SLOTS:
            send("t", (k, step - 1), t_send.at[k], t_recv.at[k, step - 1], {"x": ring("x", step)})

    def finish(k):
        total = q_own[k]
        for step in SLOTS:
            arrived("t", (k, step - 1), t_recv.at[k, step - 1])
            total += decoded(t_recv.at[k, step - 1], 256)
        for peer in range(RING):
            for h in range(2):
                row = h * 128 + peer * 32
                rows_ref[k, peer * 64 + h * 32 : peer * 64 + h * 32 + 32, :] = total[row : row + 32]

    signs_out = pltpu.make_async_copy(sg, signs_ref, sg_sem)
    swap = remote(og.at[:, mine], og.at[:, theirs], og_sem.at[1], og_sem.at[2], {"c": other})
    steps = {
        "partial_sketch": partial_sketch, "turn": turn, "sketch": sketch, "phase_one": phase_one, "relay": relay,
        "phase_two": phase_two, "phase_three": phase_three, "finish": finish,
    }
    for name, k in PLAN:
        steps[name](k)
    swap.wait_send()
    signs_out.wait()
    for kind, at in tuple(unsent):
        left(kind, at)


def reduced(sign_seed, step_number, tokens, out_grad, momentum):
    f32, bf16, i16 = jnp.float32, jnp.bfloat16, jnp.int16
    dma = pltpu.SemaphoreType.DMA
    smem = pl.BlockSpec(memory_space=pltpu.SMEM)
    anywhere = pl.BlockSpec(memory_space=pltpu.HBM)
    vmem = pl.BlockSpec(memory_space=pltpu.VMEM)
    return pl.pallas_call(
        reduce_kernel,
        out_shape=(
            jax.ShapeDtypeStruct((CHUNKS, 256, LANES), f32),
            jax.ShapeDtypeStruct((2, DIN_LOCAL, 256), bf16),
        ),
        in_specs=[smem, smem, anywhere, anywhere, anywhere],
        out_specs=(vmem, anywhere),
        scratch_shapes=[
            pltpu.VMEM((64, RANK), f32),
            pltpu.VMEM((1024, DIN_LOCAL), bf16),
            pltpu.VMEM((2, DIN_LOCAL, 256), bf16),
            pltpu.VMEM((CHUNKS, RING, QUARTER, LANES), f32),
            pltpu.VMEM((CHUNKS, 3, QUARTER + TAG, LANES), i16),
            pltpu.VMEM((CHUNKS, 3, QUARTER + TAG, LANES), i16),
            pltpu.VMEM((CHUNKS, 512, LANES), bf16),
            pltpu.VMEM((16, 512, 256), bf16),
            pltpu.VMEM((2, RING, 512, 512), bf16),
            pltpu.VMEM((CHUNKS, 2, 3, 512, LANES), f32),
            pltpu.VMEM((CHUNKS, 2, 2, 512 + TAG, LANES), i16),
            pltpu.VMEM((CHUNKS, 2, 2, 512 + TAG, LANES), i16),
            pltpu.VMEM((CHUNKS, 256, LANES), f32),
            pltpu.VMEM((CHUNKS, 2, 3, 128 + TAG, LANES), i16),
            pltpu.VMEM((CHUNKS, 2, 3, 128 + TAG, LANES), i16),
            pltpu.VMEM((CHUNKS, 2, 2, 256 + TAG, LANES), i16),
            pltpu.VMEM((CHUNKS, 2, 2, 256 + TAG, LANES), i16),
            pltpu.VMEM((CHUNKS, 256 + TAG, LANES), i16),
            pltpu.VMEM((CHUNKS, 3, 256 + TAG, LANES), i16),
            dma, dma((4,)), dma((3,)), dma,
            dma((CHUNKS, 3)), dma((CHUNKS, 3)), dma((CHUNKS,)), dma((CHUNKS,)),
            dma((CHUNKS, 2, 2)), dma((CHUNKS, 2, 2)),
            dma((CHUNKS, 2, 2)), dma((CHUNKS, 2, 2)),
            dma((CHUNKS, 2, 3)), dma((CHUNKS, 2, 3)),
            dma((CHUNKS, 3)), dma((CHUNKS, 3)),
        ],
        compiler_params=pltpu.CompilerParams(
            collective_id=0, has_side_effects=True, vmem_limit_bytes=48 * 1024 * 1024
        ),
        name="sketch_and_reduce",
    )(sign_seed, step_number, tokens, out_grad, momentum)


COLUMNS = 512


def update_kernel(rows_ref, signs_ref, weight_ref, second_ref, new_weight_ref, new_second_ref, momentum_ref, high, low):
    @pl.when(pl.program_id(0) == 0)
    def _():
        mine = pl.ds(pl.multiple_of(lax.axis_index("x") * 64, 64), 64)
        for k in range(CHUNKS):
            values = rows_ref[k]
            top = values.astype(jnp.bfloat16)
            high[:, k * LANES : (k + 1) * LANES] = top
            low[:, k * LANES : (k + 1) * LANES] = (values - top.astype(jnp.float32)).astype(jnp.bfloat16)
            momentum_ref[:, k * LANES : (k + 1) * LANES] = rows_ref[k, mine, :]

    grad = jnp.zeros((256, COLUMNS), jnp.float32)
    for part in range(2):
        at = slice(part * 256, (part + 1) * 256)
        for left in (high, low):
            grad += lax.dot_general(
                left[:, at], signs_ref[part], (((1,), (1,)), ((), ())), preferred_element_type=jnp.float32
            )
    grad = grad * (1.0 / jnp.sqrt(jnp.float32(RANK)))
    second = 0.95 * second_ref[...] + 0.05 * grad * grad
    new_second_ref[...] = second
    new_weight_ref[...] = weight_ref[...] - 0.5 * grad / (jnp.sqrt(second) + 1e-08)


def updated(rows, signs, weight, second):
    f32 = jnp.float32
    tile = pl.BlockSpec((256, COLUMNS), lambda j: (0, j))
    return pl.pallas_call(
        update_kernel,
        grid=(DIN_LOCAL // COLUMNS,),
        out_shape=(
            jax.ShapeDtypeStruct(weight.shape, f32),
            jax.ShapeDtypeStruct(second.shape, f32),
            jax.ShapeDtypeStruct((64, RANK), f32),
        ),
        in_specs=[
            pl.BlockSpec((CHUNKS, 256, LANES), lambda j: (0, 0, 0)),
            pl.BlockSpec((2, COLUMNS, 256), lambda j: (0, j, 0)),
            tile,
            tile,
        ],
        out_specs=(tile, tile, pl.BlockSpec((64, RANK), lambda j: (0, 0))),
        scratch_shapes=[pltpu.VMEM((256, RANK), jnp.bfloat16), pltpu.VMEM((256, RANK), jnp.bfloat16)],
        compiler_params=pltpu.CompilerParams(vmem_limit_bytes=32 * 1024 * 1024),
        name="dense_update",
    )(rows, signs, weight, second)


def per_device(tokens, out_grad, weight, second, momentum, sign_seed, step_number):
    rows, signs = reduced(sign_seed, step_number, tokens, out_grad, momentum)
    return updated(rows, signs, weight, second)


def solution(mesh):
    torus = Mesh(mesh.devices.reshape(4, 4, 2, mesh.shape["col"]), ("z", "y", "c", "x"))
    return jax.shard_map(
        per_device,
        mesh=torus,
        in_specs=(
            P(DP, "x"),
            P(DP_COL, None),
            P(DP, "x"),
            P(DP, "x"),
            P(DP_COL, None),
            P(),
            P(),
        ),
        out_specs=(P(DP, "x"), P(DP, "x"), P(DP_COL, None)),
        check_vma=False,
    )
```

time: 75.4 us -> 66 us (0.88); the launches traced: 75.3 us -> 64.8 us
  Pallas kernels: 72.4 us -> 61.9 us
    pallas_call x1, Pallas kernels: 67.9 us -> 57.5 us  [reduced(): pl.pallas_call(reduce_kernel, out_shape=(jax.ShapeDtypeStruct((CHUNKS, 25...]
where the time goes in v2:
time: 66 us; the launch traced here: 64.8 us
  Pallas kernels  61.9 us (94%)
  between operations  1.96 us (3%)
  local copies, waits for them, and re-layouts  0.9 us (1%)
    pallas_call x1, Pallas kernels, reduced(): pl.pallas_call(reduce_kernel, out_shape=(jax.ShapeDtypeStruct((CHUNKS, 25...  57.5 us
    pallas_call x1, Pallas kernels, updated(): pl.pallas_call(update_kernel, grid=(DIN_LOCAL // COLUMNS,), out_shape=(ja...  4.49 us

profile of v2, /device:TPU:0, one launch (start us, length us, event | category | flops | bytes accessed | tf_op | source)
XLA Modules:
  0.0 64.8 jit_solution(4705760079840819586)
XLA Ops:
  1.9 0.0 copy-start.2
  1.9 0.9 %copy-done.2 = f32[64,512]{1,0:T(8,128)S(1)} copy-done((f32[64,512]{1,0:T(8,128)S(1)}, f32[64,512]{1,0:T(8,128)}, u32[]{:S(2)}) %copy-start.2) | copy-done | bytes 131096
  2.8 0.0 copy-start
  2.8 0.0 copy-start.1
  2.8 57.5 %sketch_and_reduce.1 = (f32[4,256,128]{2,1,0:T(8,128)S(1)}, bf16[2,2048,256]{2,1,0:T(8,128)(2,1)S(1)}) custom-call(s32[1]{0:T(128)S(6)} %copy.10.seed_ref, s32[1]{0:T(128)S(6)} %copy.11.step_ref, bf16[1024,2048]{1,0:T(8,128)(2,1)} %tokens_ref.1, bf16[256,8192]{1,0:T(8,128)(2,1)} %grad_ref.1, f32[64,512]{1,0:T(8,128)S(1)} %copy-done.2), custom_call_target="tpu_custom_call" | custom-call | tf_op jit(solution)/shard_map/sketch_and_reduce/pallas_call | solution.py:312
  60.3 0.0 copy-done
  60.3 0.0 copy-done.1
  60.3 4.5 %dense_update.1 = (f32[256,2048]{1,0:T(8,128)}, f32[256,2048]{1,0:T(8,128)}, f32[64,512]{1,0:T(8,128)}) custom-call(f32[4,256,128]{2,1,0:T(8,128)S(1)} %get-tuple-element.5.rows_ref, bf16[2,2048,256]{2,1,0:T(8,128)(2,1)S(1)} %get-tuple-element.6.signs_ref, f32[256,2048]{1,0:T(8,128)S(1)} %copy-done, f32[256,2048]{1,0:T(8,128)S(1)} %copy-done.1), custom_call_target="tpu_custom_call" | custom-call | tf_op jit(solution)/shard_map/dense_update/pallas_call | solution.py:384
Async XLA Ops:
  1.9 0.9 %copy-start.2 = (f32[64,512]{1,0:T(8,128)S(1)}, f32[64,512]{1,0:T(8,128)}, u32[]{:S(2)}) copy-start(f32[64,512]{1,0:T(8,128)} %momentum_ref.1) | copy-start | bytes 393220
  2.8 57.5 %copy-start = (f32[256,2048]{1,0:T(8,128)S(1)}, f32[256,2048]{1,0:T(8,128)}, u32[]{:S(2)}) copy-start(f32[256,2048]{1,0:T(8,128)} %weight_ref.1) | copy-start | bytes 6291460
  2.8 57.5 %copy-start.1 = (f32[256,2048]{1,0:T(8,128)S(1)}, f32[256,2048]{1,0:T(8,128)}, u32[]{:S(2)}) copy-start(f32[256,2048]{1,0:T(8,128)} %second_ref.1) | copy-start | bytes 6291460

commit v3 on v2

--- a/solution.py
+++ b/solution.py
@@ -35,24 +35,24 @@
     ("phase_one", 0),
     ("sketch", 1),
     ("phase_one", 1),
+    ("relay", 0),
     ("sketch", 2),
-    ("relay", 0),
     ("phase_one", 2),
+    ("relay", 1),
     ("sketch", 3),
-    ("relay", 1),
+    ("phase_two", 0),
     ("phase_one", 3),
     ("relay", 2),
-    ("phase_two", 0),
-    ("relay", 3),
     ("phase_two", 1),
     ("phase_three", 0),
+    ("relay", 3),
     ("phase_two", 2),
     ("phase_three", 1),
     ("phase_two", 3),
     ("phase_three", 2),
+    ("phase_three", 3),
     ("finish", 0),
     ("finish", 1),
-    ("phase_three", 3),
     ("finish", 2),
     ("finish", 3),
 )
@@ -348,55 +348,68 @@
             collective_id=0, has_side_effects=True, vmem_limit_bytes=48 * 1024 * 1024
         ),
         name="sketch_and_reduce",
-    )(sign_seed, step_number, tokens, out_grad, momentum)
+    )(sign_seed, step_number, tokens, out_grad, pltpu.with_memory_space_constraint(momentum, pltpu.HBM))
 
 
 COLUMNS = 512
 
 
-def update_kernel(rows_ref, signs_ref, weight_ref, second_ref, new_weight_ref, new_second_ref, momentum_ref, high, low):
-    @pl.when(pl.program_id(0) == 0)
-    def _():
-        mine = pl.ds(pl.multiple_of(lax.axis_index("x") * 64, 64), 64)
-        for k in range(CHUNKS):
-            values = rows_ref[k]
-            top = values.astype(jnp.bfloat16)
-            high[:, k * LANES : (k + 1) * LANES] = top
-            low[:, k * LANES : (k + 1) * LANES] = (values - top.astype(jnp.float32)).astype(jnp.bfloat16)
-            momentum_ref[:, k * LANES : (k + 1) * LANES] = rows_ref[k, mine, :]
-
-    grad = jnp.zeros((256, COLUMNS), jnp.float32)
-    for part in range(2):
-        at = slice(part * 256, (part + 1) * 256)
-        for left in (high, low):
-            grad += lax.dot_general(
-                left[:, at], signs_ref[part], (((1,), (1,)), ((), ())), preferred_element_type=jnp.float32
-            )
-    grad = grad * (1.0 / jnp.sqrt(jnp.float32(RANK)))
-    second = 0.95 * second_ref[...] + 0.05 * grad * grad
-    new_second_ref[...] = second
-    new_weight_ref[...] = weight_ref[...] - 0.5 * grad / (jnp.sqrt(second) + 1e-08)
+def update_kernel(
+    rows_ref, signs_ref, weight_ref, second_ref, new_weight_ref, new_second_ref, momentum_ref,
+    high, low, weight_out, second_out, weight_sem, second_sem,
+):
+    for k in range(CHUNKS):
+        values = rows_ref[k]
+        top = values.astype(jnp.bfloat16)
+        high[:, k * LANES : (k + 1) * LANES] = top
+        low[:, k * LANES : (k + 1) * LANES] = (values - top.astype(jnp.float32)).astype(jnp.bfloat16)
+    copies = []
+    for tile in range(DIN_LOCAL // COLUMNS):
+        at = slice(tile * COLUMNS, (tile + 1) * COLUMNS)
+        grad = jnp.zeros((256, COLUMNS), jnp.float32)
+        for part in range(2):
+            inner = slice(part * 256, (part + 1) * 256)
+            for left in (high, low):
+                grad += lax.dot_general(
+                    left[:, inner], signs_ref[part, at, :], (((1,), (1,)), ((), ())), preferred_element_type=jnp.float32
+                )
+        grad = grad * (1.0 / jnp.sqrt(jnp.float32(RANK)))
+        second = 0.95 * second_ref[:, at] + 0.05 * grad * grad
+        second_out[tile] = second
+        copies.append(pltpu.make_async_copy(second_out.at[tile], new_second_ref.at[:, at], second_sem.at[tile]))
+        copies[-1].start()
+        weight_out[tile] = weight_ref[:, at] - 0.5 * grad / (jnp.sqrt(second) + 1e-08)
+        copies.append(pltpu.make_async_copy(weight_out.at[tile], new_weight_ref.at[:, at], weight_sem.at[tile]))
+        copies[-1].start()
+    mine = pl.ds(pl.multiple_of(lax.axis_index("x") * 64, 64), 64)
+    for k in range(CHUNKS):
+        momentum_ref[:, k * LANES : (k + 1) * LANES] = rows_ref[k, mine, :]
+    for copy in copies:
+        copy.wait()
 
 
 def updated(rows, signs, weight, second):
     f32 = jnp.float32
-    tile = pl.BlockSpec((256, COLUMNS), lambda j: (0, j))
+    tiles = DIN_LOCAL // COLUMNS
+    vmem = pl.BlockSpec(memory_space=pltpu.VMEM)
+    hbm = pl.BlockSpec(memory_space=pltpu.HBM)
     return pl.pallas_call(
         update_kernel,
-        grid=(DIN_LOCAL // COLUMNS,),
         out_shape=(
             jax.ShapeDtypeStruct(weight.shape, f32),
             jax.ShapeDtypeStruct(second.shape, f32),
             jax.ShapeDtypeStruct((64, RANK), f32),
         ),
-        in_specs=[
-            pl.BlockSpec((CHUNKS, 256, LANES), lambda j: (0, 0, 0)),
-            pl.BlockSpec((2, COLUMNS, 256), lambda j: (0, j, 0)),
-            tile,
-            tile,
+        in_specs=[vmem, vmem, vmem, vmem],
+        out_specs=(hbm, hbm, vmem),
+        scratch_shapes=[
+            pltpu.VMEM((256, RANK), jnp.bfloat16),
+            pltpu.VMEM((256, RANK), jnp.bfloat16),
+            pltpu.VMEM((tiles, 256, COLUMNS), f32),
+            pltpu.VMEM((tiles, 256, COLUMNS), f32),
+            pltpu.SemaphoreType.DMA((tiles,)),
+            pltpu.SemaphoreType.DMA((tiles,)),
         ],
-        out_specs=(tile, tile, pl.BlockSpec((64, RANK), lambda j: (0, 0))),
-        scratch_shapes=[pltpu.VMEM((256, RANK), jnp.bfloat16), pltpu.VMEM((256, RANK), jnp.bfloat16)],
         compiler_params=pltpu.CompilerParams(vmem_limit_bytes=32 * 1024 * 1024),
         name="dense_update",
     )(rows, signs, weight, second)

time: 66 us -> 61.3 us (0.929); the launches traced: 64.8 us -> 61.1 us
  Pallas kernels: 61.9 us -> 59 us
  local copies, waits for them, and re-layouts: 0.9 us -> 0.01 us
    pallas_call x1, Pallas kernels: 57.5 us -> 55.3 us  [reduced(): pl.pallas_call(reduce_kernel, out_shape=(jax.ShapeDtypeStruct((CHUNKS, 25...]
    unnamed x6 -> x4, local copies, waits for them, and re-layouts: 0.9 us -> 0.01 us
    pallas_call x1, Pallas kernels: 4.49 us -> 3.73 us  [updated(): pl.pallas_call(update_kernel, out_shape=(jax.ShapeDtypeStruct(weight.shap...]
where the time goes in v3:
time: 61.3 us; the launch traced here: 61.1 us
  Pallas kernels  59 us (96%)
  between operations  2.12 us (3%)
    pallas_call x1, Pallas kernels, reduced(): pl.pallas_call(reduce_kernel, out_shape=(jax.ShapeDtypeStruct((CHUNKS, 25...  55.3 us
    pallas_call x1, Pallas kernels, updated(): pl.pallas_call(update_kernel, out_shape=(jax.ShapeDtypeStruct(weight.shap...  3.73 us

profile of v3, /device:TPU:0, one launch (start us, length us, event | category | flops | bytes accessed | tf_op | source)
XLA Modules:
  0.0 61.1 jit_solution(9741146408834025647)
XLA Ops:
  1.9 0.0 copy-start
  1.9 0.0 copy-start.1
  1.9 55.3 %sketch_and_reduce.1 = (f32[4,256,128]{2,1,0:T(8,128)S(1)}, bf16[2,2048,256]{2,1,0:T(8,128)(2,1)S(1)}) custom-call(s32[1]{0:T(128)S(6)} %copy.10.seed_ref, s32[1]{0:T(128)S(6)} %copy.11.step_ref, bf16[1024,2048]{1,0:T(8,128)(2,1)} %tokens_ref.1, bf16[256,8192]{1,0:T(8,128)(2,1)} %grad_ref.1, f32[64,512]{1,0:T(8,128)} %momentum_ref.1), custom_call_target="tpu_custom_call" | custom-call | tf_op jit(solution)/shard_map/sketch_and_reduce/pallas_call | solution.py:312
  57.2 0.0 copy-done
  57.2 0.0 copy-done.1
  57.3 3.7 %dense_update.1 = (f32[256,2048]{1,0:T(8,128)}, f32[256,2048]{1,0:T(8,128)}, f32[64,512]{1,0:T(8,128)}) custom-call(f32[4,256,128]{2,1,0:T(8,128)S(1)} %get-tuple-element.5.rows_ref, bf16[2,2048,256]{2,1,0:T(8,128)(2,1)S(1)} %get-tuple-element.6.signs_ref, f32[256,2048]{1,0:T(8,128)S(1)} %copy-done, f32[256,2048]{1,0:T(8,128)S(1)} %copy-done.1), custom_call_target="tpu_custom_call" | custom-call | tf_op jit(solution)/shard_map/dense_update/pallas_call | solution.py:396
Async XLA Ops:
  1.9 55.3 %copy-start = (f32[256,2048]{1,0:T(8,128)S(1)}, f32[256,2048]{1,0:T(8,128)}, u32[]{:S(2)}) copy-start(f32[256,2048]{1,0:T(8,128)} %weight_ref.1) | copy-start | bytes 6291460
  1.9 55.3 %copy-start.1 = (f32[256,2048]{1,0:T(8,128)S(1)}, f32[256,2048]{1,0:T(8,128)}, u32[]{:S(2)}) copy-start(f32[256,2048]{1,0:T(8,128)} %second_ref.1) | copy-start | bytes 6291460

commit v4 on v3

--- a/solution.py
+++ b/solution.py
@@ -53,7 +53,9 @@
     ("phase_three", 3),
     ("finish", 0),
     ("finish", 1),
+    ("dense", 0),
     ("finish", 2),
+    ("dense", 1),
     ("finish", 3),
 )
 
@@ -105,9 +107,18 @@
     lax.fori_loop(0, out_ref.shape[1] // HASH_ROWS, body, 0)
 
 
+def halves(values):
+    top = values.astype(jnp.bfloat16)
+    return top, (values - top.astype(jnp.float32)).astype(jnp.bfloat16)
+
+
+def times_signs(left, signs):
+    return lax.dot_general(left, signs, (((1,), (1,)), ((), ())), preferred_element_type=jnp.float32)
+
+
 def reduce_kernel(
     seed_ref, step_ref, tokens_ref, grad_ref, momentum_ref,
-    rows_ref, signs_ref,
+    rows_ref, signs_ref, dense_ref,
     old, tok, sg, s_own, s_send, s_recv, sk, og, og_t,
     p_own, p_send, p_recv, q_own, q_send, q_recv, u_send, u_recv, t_send, t_recv,
     old_sem, tok_sem, og_sem, sg_sem, s_ss, s_rs, sk_ss, sk_rs,
@@ -289,11 +300,28 @@
                 row = h * 128 + peer * 32
                 rows_ref[k, peer * 64 + h * 32 : peer * 64 + h * 32 + 32, :] = total[row : row + 32]
 
-    signs_out = pltpu.make_async_copy(sg, signs_ref, sg_sem)
+    def dense(part):
+        chunks = ((0, 1), (2,))[part]
+        inner = slice(0, len(chunks) * LANES)
+        pairs = [halves(rows_ref[k]) for k in chunks]
+        top = jnp.concatenate([pair[0] for pair in pairs], axis=1)
+        rest = jnp.concatenate([pair[1] for pair in pairs], axis=1)
+
+        def body(tile, carry):
+            at = pl.ds(pl.multiple_of(tile * 512, 512), 512)
+            grad = times_signs(top, sg[part, at, inner]) + times_signs(rest, sg[part, at, inner])
+            if part:
+                grad += dense_ref[tile]
+            dense_ref[tile] = grad
+            return carry
+
+        lax.fori_loop(0, DIN_LOCAL // 512, body, 0)
+
+    signs_out = pltpu.make_async_copy(sg.at[1, :, LANES:], signs_ref, sg_sem)
     swap = remote(og.at[:, mine], og.at[:, theirs], og_sem.at[1], og_sem.at[2], {"c": other})
     steps = {
         "partial_sketch": partial_sketch, "turn": turn, "sketch": sketch, "phase_one": phase_one, "relay": relay,
-        "phase_two": phase_two, "phase_three": phase_three, "finish": finish,
+        "phase_two": phase_two, "phase_three": phase_three, "finish": finish, "dense": dense,
     }
     for name, k in PLAN:
         steps[name](k)
@@ -313,10 +341,11 @@
         reduce_kernel,
         out_shape=(
             jax.ShapeDtypeStruct((CHUNKS, 256, LANES), f32),
-            jax.ShapeDtypeStruct((2, DIN_LOCAL, 256), bf16),
+            jax.ShapeDtypeStruct((DIN_LOCAL, LANES), bf16),
+            jax.ShapeDtypeStruct((DIN_LOCAL // 512, 256, 512), f32),
         ),
         in_specs=[smem, smem, anywhere, anywhere, anywhere],
-        out_specs=(vmem, anywhere),
+        out_specs=(vmem, anywhere, vmem),
         scratch_shapes=[
             pltpu.VMEM((64, RANK), f32),
             pltpu.VMEM((1024, DIN_LOCAL), bf16),
@@ -355,24 +384,14 @@
 
 
 def update_kernel(
-    rows_ref, signs_ref, weight_ref, second_ref, new_weight_ref, new_second_ref, momentum_ref,
-    high, low, weight_out, second_out, weight_sem, second_sem,
+    rows_ref, signs_ref, dense_ref, weight_ref, second_ref, new_weight_ref, new_second_ref, momentum_ref,
+    weight_out, second_out, weight_sem, second_sem,
 ):
-    for k in range(CHUNKS):
-        values = rows_ref[k]
-        top = values.astype(jnp.bfloat16)
-        high[:, k * LANES : (k + 1) * LANES] = top
-        low[:, k * LANES : (k + 1) * LANES] = (values - top.astype(jnp.float32)).astype(jnp.bfloat16)
+    top, rest = halves(rows_ref[CHUNKS - 1])
     copies = []
     for tile in range(DIN_LOCAL // COLUMNS):
         at = slice(tile * COLUMNS, (tile + 1) * COLUMNS)
-        grad = jnp.zeros((256, COLUMNS), jnp.float32)
-        for part in range(2):
-            inner = slice(part * 256, (part + 1) * 256)
-            for left in (high, low):
-                grad += lax.dot_general(
-                    left[:, inner], signs_ref[part, at, :], (((1,), (1,)), ((), ())), preferred_element_type=jnp.float32
-                )
+        grad = dense_ref[tile] + times_signs(top, signs_ref[at, :]) + times_signs(rest, signs_ref[at, :])
         grad = grad * (1.0 / jnp.sqrt(jnp.float32(RANK)))
         second = 0.95 * second_ref[:, at] + 0.05 * grad * grad
         second_out[tile] = second
@@ -388,7 +407,7 @@
         copy.wait()
 
 
-def updated(rows, signs, weight, second):
+def updated(rows, signs, dense, weight, second):
     f32 = jnp.float32
     tiles = DIN_LOCAL // COLUMNS
     vmem = pl.BlockSpec(memory_space=pltpu.VMEM)
@@ -400,11 +419,9 @@
             jax.ShapeDtypeStruct(second.shape, f32),
             jax.ShapeDtypeStruct((64, RANK), f32),
         ),
-        in_specs=[vmem, vmem, vmem, vmem],
+        in_specs=[vmem, vmem, vmem, vmem, vmem],
         out_specs=(hbm, hbm, vmem),
         scratch_shapes=[
-            pltpu.VMEM((256, RANK), jnp.bfloat16),
-            pltpu.VMEM((256, RANK), jnp.bfloat16),
             pltpu.VMEM((tiles, 256, COLUMNS), f32),
             pltpu.VMEM((tiles, 256, COLUMNS), f32),
             pltpu.SemaphoreType.DMA((tiles,)),
@@ -412,12 +429,12 @@
         ],
         compiler_params=pltpu.CompilerParams(vmem_limit_bytes=32 * 1024 * 1024),
         name="dense_update",
-    )(rows, signs, weight, second)
+    )(rows, signs, dense, weight, second)
 
 
 def per_device(tokens, out_grad, weight, second, momentum, sign_seed, step_number):
-    rows, signs = reduced(sign_seed, step_number, tokens, out_grad, momentum)
-    return updated(rows, signs, weight, second)
+    rows, signs, dense = reduced(sign_seed, step_number, tokens, out_grad, momentum)
+    return updated(rows, signs, dense, weight, second)
 
 
 def solution(mesh):

time: 61.3 us -> 60.8 us (level)
  no operation moved by 1% of the time
where the time goes in v4:
time: 60.8 us; the launch traced here: 60.7 us
  Pallas kernels  58.5 us (96%)
  between operations  2.12 us (3%)
    pallas_call x1, Pallas kernels, reduced(): pl.pallas_call(reduce_kernel, out_shape=(jax.ShapeDtypeStruct((CHUNKS, 25...  55.2 us
    pallas_call x1, Pallas kernels, updated(): pl.pallas_call(update_kernel, out_shape=(jax.ShapeDtypeStruct(weight.shap...  3.3 us

profile of v4, /device:TPU:0, one launch (start us, length us, event | category | flops | bytes accessed | tf_op | source)
XLA Modules:
  0.0 60.7 jit_solution(1756477964562609766)
XLA Ops:
  1.9 0.0 copy-start
  1.9 0.0 copy-start.1
  1.9 55.2 %sketch_and_reduce.1 = (f32[4,256,128]{2,1,0:T(8,128)S(1)}, bf16[2048,128]{1,0:T(8,128)(2,1)S(1)}, f32[4,256,512]{2,1,0:T(8,128)S(1)}) custom-call(s32[1]{0:T(128)S(6)} %copy.10.seed_ref, s32[1]{0:T(128)S(6)} %copy.11.step_ref, bf16[1024,2048]{1,0:T(8,128)(2,1)} %tokens_ref.1, bf16[256,8192]{1,0:T(8,128)(2,1)} %grad_ref.1, f32[64,512]{1,0:T(8,128)} %momentum_ref.1), custom_call_target="tpu_custom_call" | custom-call | tf_op jit(solution)/shard_map/sketch_and_reduce/pallas_call | solution.py:340
  57.2 0.0 copy-done
  57.2 0.0 copy-done.1
  57.2 3.3 %dense_update.1 = (f32[256,2048]{1,0:T(8,128)}, f32[256,2048]{1,0:T(8,128)}, f32[64,512]{1,0:T(8,128)}) custom-call(f32[4,256,128]{2,1,0:T(8,128)S(1)} %get-tuple-element.6.rows_ref, bf16[2048,128]{1,0:T(8,128)(2,1)S(1)} %get-tuple-element.7.signs_ref, f32[4,256,512]{2,1,0:T(8,128)S(1)} %get-tuple-element.8.dense_ref, f32[256,2048]{1,0:T(8,128)S(1)} %copy-done, ...), custom_call_target="tpu_custom_call" | custom-call | tf_op jit(solution)/shard_map/dense_update/pallas_call | solution.py:415
Async XLA Ops:
  1.9 55.3 %copy-start = (f32[256,2048]{1,0:T(8,128)S(1)}, f32[256,2048]{1,0:T(8,128)}, u32[]{:S(2)}) copy-start(f32[256,2048]{1,0:T(8,128)} %weight_ref.1) | copy-start | bytes 6291460
  1.9 55.3 %copy-start.1 = (f32[256,2048]{1,0:T(8,128)S(1)}, f32[256,2048]{1,0:T(8,128)}, u32[]{:S(2)}) copy-start(f32[256,2048]{1,0:T(8,128)} %second_ref.1) | copy-start | bytes 6291460

commit v5 on v4

--- a/solution.py
+++ b/solution.py
@@ -14,7 +14,7 @@
 RANK = 512
 CHUNKS = 4
 LANES = 128
-TAG = 16
+TAG = 8
 DIN_LOCAL = 2048
 QUARTER = 256
 TOKENS = 32768

time: 60.8 us -> 60.2 us (level)
  no operation moved by 1% of the time
where the time goes in v5:
time: 60.2 us; the launch traced here: 60.1 us
  Pallas kernels  58 us (96%)
  between operations  2.12 us (4%)
    pallas_call x1, Pallas kernels, reduced(): pl.pallas_call(reduce_kernel, out_shape=(jax.ShapeDtypeStruct((CHUNKS, 25...  54.7 us
    pallas_call x1, Pallas kernels, updated(): pl.pallas_call(update_kernel, out_shape=(jax.ShapeDtypeStruct(weight.shap...  3.3 us

profile of v5, /device:TPU:0, one launch (start us, length us, event | category | flops | bytes accessed | tf_op | source)
XLA Modules:
  0.0 60.1 jit_solution(6938529927388576483)
XLA Ops:
  1.9 0.0 copy-start
  1.9 0.0 copy-start.1
  1.9 54.7 %sketch_and_reduce.1 = (f32[4,256,128]{2,1,0:T(8,128)S(1)}, bf16[2048,128]{1,0:T(8,128)(2,1)S(1)}, f32[4,256,512]{2,1,0:T(8,128)S(1)}) custom-call(s32[1]{0:T(128)S(6)} %copy.10.seed_ref, s32[1]{0:T(128)S(6)} %copy.11.step_ref, bf16[1024,2048]{1,0:T(8,128)(2,1)} %tokens_ref.1, bf16[256,8192]{1,0:T(8,128)(2,1)} %grad_ref.1, f32[64,512]{1,0:T(8,128)} %momentum_ref.1), custom_call_target="tpu_custom_call" | custom-call | tf_op jit(solution)/shard_map/sketch_and_reduce/pallas_call | solution.py:340
  56.6 0.0 copy-done
  56.6 0.0 copy-done.1
  56.6 3.3 %dense_update.1 = (f32[256,2048]{1,0:T(8,128)}, f32[256,2048]{1,0:T(8,128)}, f32[64,512]{1,0:T(8,128)}) custom-call(f32[4,256,128]{2,1,0:T(8,128)S(1)} %get-tuple-element.6.rows_ref, bf16[2048,128]{1,0:T(8,128)(2,1)S(1)} %get-tuple-element.7.signs_ref, f32[4,256,512]{2,1,0:T(8,128)S(1)} %get-tuple-element.8.dense_ref, f32[256,2048]{1,0:T(8,128)S(1)} %copy-done, ...), custom_call_target="tpu_custom_call" | custom-call | tf_op jit(solution)/shard_map/dense_update/pallas_call | solution.py:415
Async XLA Ops:
  1.9 54.7 %copy-start = (f32[256,2048]{1,0:T(8,128)S(1)}, f32[256,2048]{1,0:T(8,128)}, u32[]{:S(2)}) copy-start(f32[256,2048]{1,0:T(8,128)} %weight_ref.1) | copy-start | bytes 6291460
  1.9 54.7 %copy-start.1 = (f32[256,2048]{1,0:T(8,128)S(1)}, f32[256,2048]{1,0:T(8,128)}, u32[]{:S(2)}) copy-start(f32[256,2048]{1,0:T(8,128)} %second_ref.1) | copy-start | bytes 6291460
